TPU v7x, 256 devices: a whole 4x4x8 slice. The times are simulated.
256 devices in a mesh: heads: 8 (over z), tokens: 32 (over x, y, core).
Axes of the slice: x: 4, y: 4, z: 8, core: 2. Of those that a mesh axis runs over, the one named last changes fastest.
Arguments:
- hidden_in: bfloat16 [8192, 5120], P('tokens', 'heads'), may hold values from -4 to 4
- queries: bfloat16 [8192, 5120], P('tokens', 'heads'), may hold values from -7 to 7
- keyvals: bfloat16 [8192, 2, 1024], P('tokens', None, 'heads'), may hold values from -6 to 6
- out_weight: bfloat16 [5120, 5120], P('heads', 'tokens'), may hold values from -0.01953125 to 0.01953125
- kv_gain: bfloat16 [5120], P('heads'), may hold values from 0.099609375 to 1.8984375
- kv_weight: bfloat16 [5120, 2, 1024], P(None, None, 'heads'), may hold values from -0.25 to 0.25
- cache: bfloat16 [131072, 2, 1024], P('tokens', None, 'heads'), may hold values from -12 to 12
- page_home: int32 [512], replicated, may hold values from 0 to 8191, as said below
- cache_len: int32 [1], replicated, may hold values from 16384 to 65536
- beam_state: bfloat16 [256, 5120], P(None, 'tokens'), may hold values from -4 to 4
- parents: int32 [256], replicated, may hold values from 0 to 255
- beam_gain: bfloat16 [2, 5120], P(None, 'tokens'), may hold values from 0.099609375 to 1.8984375
- query_weight: bfloat16 [2, 5120, 5120], P(None, 'tokens', 'heads'), may hold values from -1 to 1
- beam_out_weight: bfloat16 [2, 5120, 5120], P(None, 'heads', 'tokens'), may hold values from -0.078125 to 0.078125
Outputs:
- stretch_hidden: bfloat16 [8192, 5120], P('tokens', 'heads')
- new_cache: bfloat16 [131072, 2, 1024], P('tokens', None, 'heads')
- beams_out: bfloat16 [256, 5120], P(None, 'tokens')
Inputs may be any that keep to these rules, and one draw needn't show every extreme that they name: Prefill page p overwrites a page held by index (p + c) mod 32 of tokens, i.e. page_home[p] // 256 equals it, for one c of each draw; all entries differ.
All inputs are finite; a program needn't handle non-finite values.
Results may differ from a plain program's by a relative error of at most 0.023.
Values may be sent and summed in bfloat16 or wider, within the bound.
A program may use at most 128 MiB of HBM per device.

v0:
```python
import functools
import math

import jax
import jax.numpy as jnp
from jax import lax
from jax.experimental import pallas as pl
from jax.experimental.pallas import tpu as pltpu
from jax.sharding import PartitionSpec as P

D = 5120
DH = 128
WINDOW = 1024
PAGE = 16
LAYERS = 2
EPSILON = 1e-06
SCALE = DH ** (-0.5)
SCALE2 = SCALE * math.log2(math.e)
MESH = pl.DeviceIdType.MESH
VMEM_SPEC = pl.BlockSpec(memory_space=pltpu.VMEM)


def scatter_start(send, recv, sems, axis, count, me):
    def one(step, carry):
        peer = lax.rem(me + step, count)
        pltpu.make_async_remote_copy(
            src_ref=send.at[peer],
            dst_ref=recv.at[me],
            send_sem=sems.at[0],
            recv_sem=sems.at[1],
            device_id={axis: peer},
            device_id_type=MESH,
        ).start()
        return carry

    lax.fori_loop(1, count, one, 0)


def gather_start(held, sems, axis, count, me):
    def one(step, carry):
        peer = lax.rem(me + step, count)
        pltpu.make_async_remote_copy(
            src_ref=held.at[me],
            dst_ref=held.at[me],
            send_sem=sems.at[0],
            recv_sem=sems.at[1],
            device_id={axis: peer},
            device_id_type=MESH,
        ).start()
        return carry

    lax.fori_loop(1, count, one, 0)


def finish(held, sems, axis, count, me):
    everything = held.at[pl.ds(0, count - 1)]
    pltpu.make_async_remote_copy(
        src_ref=everything,
        dst_ref=everything,
        send_sem=sems.at[0],
        recv_sem=sems.at[1],
        device_id={axis: lax.rem(me + 1, count)},
        device_id_type=MESH,
    ).wait()


def greet(axis, count, me):
    barrier = pltpu.get_barrier_semaphore()

    def one(step, carry):
        pl.semaphore_signal(
            barrier, inc=1, device_id={axis: lax.rem(me + step, count)}, device_id_type=MESH
        )
        return carry

    lax.fori_loop(1, count, one, 0)


def page_slot(home_ref, me, own_pages, pages_here, n_tok, slot):
    shift = lax.div(home_ref[0], pages_here)
    which = lax.rem(me - shift - own_pages * slot + 2 * n_tok * own_pages, n_tok)
    page = home_ref[own_pages * slot + jnp.minimum(which, own_pages - 1)]
    return jnp.where(which < own_pages, lax.rem(page, pages_here), -1)


def whole_kernel(
    n_tok,
    n_head,
    side,
    subs,
    subs2,
    block,
    split_at,
    home_hbm,
    len_hbm,
    parents_hbm,
    query_hbm,
    hid_hbm,
    gain_hbm,
    beams_hbm,
    beam_gain_hbm,
    own_w,
    own_kv,
    kvw,
    cache,
    wo_hbm,
    wq_hbm,
    hid_out_hbm,
    inbox_hbm,
    state_out_hbm,
    state_end,
    hid_out_ref,
    home_ref,
    len_ref,
    parents_ref,
    query_ref,
    hid_ref,
    gain_ref,
    beams_ref,
    beam_gain_ref,
    whole_w,
    win,
    win_k,
    win_v,
    att,
    state_ref,
    cache_v,
    part,
    s_buf,
    r_buf,
    part2,
    s_buf2,
    r_buf2,
    squares,
    kvr,
    kvd,
    spread,
    keys,
    values,
    wo,
    wq,
    bias,
    acc_s,
    top_s,
    fk,
    fv,
    pages,
    outbox,
    inbox,
    lse_s,
    oa_send,
    ob_send,
    oa_recv,
    ob_recv,
    oa_held,
    ob_held,
    b_send,
    b_recv,
    s_held,
    q_send,
    q_recv,
    qa_held,
    qb_held,
    q0_held,
    local_sems,
    in_sems,
    w_sems,
    pair_sems,
    win_sems,
    kv_sems,
    kv_pair_sems,
    s_sems,
    r_sems,
    s_sems2,
    r_sems2,
    sq_sems,
    page_sems,
    tok_sems,
    head_sems,
):
    f32, bf16 = jnp.float32, jnp.bfloat16
    me = lax.axis_index("tokens")
    me_h = lax.axis_index("heads")
    tok = ("tokens", n_tok, me)
    head = ("heads", n_head, me_h)
    core = lax.rem(me, 2)
    y = lax.rem(me // 2, side)
    x = me // (2 * side)
    wide = n_tok // (2 * side)
    partner = me + 1 - 2 * core
    at = lambda i, j: (
        lax.rem(x + i + 2 * wide, wide) * side + lax.rem(y + j + 2 * side, side)
    ) * 2 + core
    cache_in = pltpu.make_async_copy(cache, cache_v, local_sems.at[3])
    wq_in = pltpu.make_async_copy(wq_hbm, wq, local_sems.at[0])
    wo_in = pltpu.make_async_copy(
        wo_hbm, wo.at[:, pl.ds(0, wo_hbm.shape[1])], local_sems.at[4]
    )
    small_in = [
        pltpu.make_async_copy(src, dst, in_sems.at[k])
        for k, (src, dst) in enumerate(
            [
                (parents_hbm, parents_ref),
                (beams_hbm, beams_ref.at[pl.ds(0, beams_hbm.shape[0])]),
                (beam_gain_hbm, beam_gain_ref),
                (home_hbm, home_ref),
                (len_hbm, len_ref),
                (query_hbm, query_ref),
                (hid_hbm, hid_ref),
                (gain_hbm, gain_ref),
            ]
        )
    ]
    for copy in small_in[:3]:
        copy.start()
    wq_in.start()
    for copy in small_in[3:]:
        copy.start()
    cache_in.start()
    wo_in.start()
    greet(*tok)
    greet(*head)

    tokens, width = hid_ref.shape
    beams = beams_hbm.shape[1]
    beams_ref[beams_hbm.shape[0] :] = jnp.zeros((beams_ref.shape[0] - beams_hbm.shape[0], beams), bf16)
    wo[:, wo_hbm.shape[1] :] = jnp.zeros((LAYERS, wo.shape[1] - wo_hbm.shape[1], width), bf16)
    source = lax.broadcasted_iota(jnp.int32, (beams, beams), 0)
    for copy in small_in[:3]:
        copy.wait()
    picked = jnp.transpose(jnp.where(source == parents_ref[...], 1.0, 0.0).astype(f32))
    picked = picked.astype(bf16)
    cols = wq.shape[1]
    extra = cols - DH
    strips = DH // extra

    def both_of(lhs, ref, lead):
        first = ref[lead, :DH] if lead is not None else ref[:DH]
        other = ref[lead, DH:] if lead is not None else ref[DH:]
        dims = (((1,), (1,)), ((), ()))
        return (
            lax.dot_general(lhs, first, dims, preferred_element_type=f32),
            lax.dot_general(lhs, other, dims, preferred_element_type=f32),
        )

    def pack(ref, main, rest):
        high = beams // n_head
        ref[:, :high, :] = main.reshape(n_head, high, DH).astype(bf16)
        strip = rest.reshape(n_head, strips, high // strips, DH)
        total = strip[:, 0]
        for k in range(1, strips):
            total = total + pltpu.roll(strip[:, k], k * extra, 2)
        ref[:, high:, :] = total.astype(bf16)

    def unpack(value):
        high = beams // n_head
        main = value[:, :high].reshape(beams, DH)
        strip = value[:, high:]
        inside = lax.broadcasted_iota(jnp.int32, strip.shape, 2) < extra
        parts = [
            jnp.where(inside, pltpu.roll(strip, (DH - k * extra) % DH, 2), 0.0)
            for k in range(strips)
        ]
        return main, jnp.stack(parts, axis=1).reshape(beams, DH)

    state = both_of(picked, beams_ref, None)
    pack(state_ref, *state)
    wq_in.wait()

    def send_query(layer, state):
        main, rest = state
        sq = jnp.sum(main * main + rest * rest, axis=1, keepdims=True)
        gain = beam_gain_ref[layer : layer + 1, :].astype(f32)
        share_q = jnp.dot(
            (main * gain[:, :DH]).astype(bf16), wq[layer, :DH], preferred_element_type=f32
        ) + jnp.dot(
            (rest[:, :extra] * gain[:, DH:]).astype(bf16), wq[layer, DH:], preferred_element_type=f32
        )
        rows = beams // n_tok
        q_send[layer, :, :, :width] = share_q.reshape(n_tok, rows, width).astype(bf16)
        q_send[layer, :, :, width:] = (
            jnp.broadcast_to(sq, (beams, DH)).reshape(n_tok, rows, DH).astype(bf16)
        )
        return lambda: scatter_start(q_send.at[layer], q_recv.at[layer], tok_sems.at[2 + layer, 0], *tok)

    def sum_query(layer):
        recv = q_recv.at[layer]
        recv[me] = q_send[layer, me]
        finish(recv, tok_sems.at[2 + layer, 0], *tok)
        total = jnp.sum(recv[...].astype(f32), axis=0)
        scale = lax.rsqrt(total[:, width : width + 1] / D + EPSILON)
        return (total[:, :width] * scale).astype(bf16)

    start_query = send_query(0, state)

    cache_rows = keys.shape[0]
    pages_here = cache_rows // PAGE
    own_pages = tokens // PAGE
    lane = lax.broadcasted_iota(jnp.int32, (1, cache_rows), 1)
    for copy in small_in[3:]:
        copy.wait()
    kept = (me * cache_rows + lane) < len_ref[0]
    page_of = lane // PAGE
    for slot in range(n_tok):
        landing = page_slot(home_ref, me, own_pages, pages_here, n_tok, slot)
        kept = kept & (page_of != landing)
    bias[...] = jnp.where(kept, 0.0, -1e30).astype(f32)

    pl.semaphore_wait(pltpu.get_barrier_semaphore(), n_tok + n_head - 2)
    start_query()

    def remote(src, dst, sems, target, axis="tokens"):
        return pltpu.make_async_remote_copy(
            src_ref=src,
            dst_ref=dst,
            send_sem=sems.at[0],
            recv_sem=sems.at[1],
            device_id={axis: target},
            device_id_type=MESH,
        )

    back = lambda b: lax.rem(me - b + n_tok, n_tok)
    ahead = lambda b: lax.rem(me + b, n_tok)
    win_two = remote(own_kv, win.at[2], win_sems.at[0], ahead(2))
    win_four = remote(own_kv, win.at[4], win_sems.at[1], ahead(4))
    win_two.start()
    win_four.start()

    depth = own_w.shape[0]
    cut_w = depth * 2 // 5
    spot = lambda half, i, j: at(i, j) if half == 0 else at(j, i)

    def rows_of(half, stage=None, part_at=None):
        begin, size = (0, cut_w) if half == 0 else (cut_w, depth - cut_w)
        if part_at is None:
            return pl.ds(begin, size)
        up = size // 2 if half == stage else 16
        return pl.ds(begin, up) if part_at == 0 else pl.ds(begin + up, size - up)

    slots = {}
    for half in (0, 1):
        for name in ("a+", "a-", "f+", "f-"):
            slots[half, name] = len(slots)
        for i in (0, -1, 1, 2):
            for name in ("a+", "a-", "f+", "f-"):
                slots[half, i, name] = len(slots)

    def first(half, name):
        way = 1 if name[1] == "+" else -1
        target = spot(half, way, 0)
        if name[0] == "a":
            where = rows_of(half)
            return remote(
                own_w.at[where], whole_w.at[me, where], w_sems.at[slots[half, name]], target
            )
        ref = whole_w.at[spot(half, -way, 0), rows_of(half, 0, 0 if way == 1 else 1)]
        return remote(ref, ref, w_sems.at[slots[half, name]], target)

    def first_in(half, name):
        way = 1 if name[1] == "+" else -1
        if name[0] == "a":
            ref = whole_w.at[spot(half, -way, 0), rows_of(half)]
        else:
            ref = whole_w.at[spot(half, -2 * way, 0), rows_of(half, 0, 0 if way == 1 else 1)]
        return remote(ref, ref, w_sems.at[slots[half, name]], spot(half, way, 0))

    def second(half, i, name):
        way = 1 if name[1] == "+" else -1
        target = spot(half, 0, way)
        if name[0] == "a":
            where = rows_of(half)
            dst = whole_w.at[spot(half, i, 0), where]
            src = own_w.at[where] if i == 0 else dst
        else:
            src = dst = whole_w.at[spot(half, i, -way), rows_of(half, 1, 0 if way == 1 else 1)]
        return remote(src, dst, w_sems.at[slots[half, i, name]], target)

    def second_in(half, i, name):
        way = 1 if name[1] == "+" else -1
        if name[0] == "a":
            ref = whole_w.at[spot(half, i, -way), rows_of(half)]
        else:
            ref = whole_w.at[spot(half, i, -2 * way), rows_of(half, 1, 0 if way == 1 else 1)]
        return remote(ref, ref, w_sems.at[slots[half, i, name]], spot(half, 0, way))

    def share(half, i, j):
        where = rows_of(half)
        dst = whole_w.at[spot(half, i, j), where]
        src = own_w.at[where] if (i, j) == (0, 0) else dst
        remote(src, dst, pair_sems, partner).start()

    halves = (0, 1)
    for half in halves:
        for name in ("a+", "a-"):
            first(half, name).start()
    for half in halves:
        for name in ("a+", "a-"):
            second(half, 0, name).start()
    for half in halves:
        share(half, 0, 0)

    kv_rows = kvw.shape[1] // 2
    kv_half = pl.ds(pl.multiple_of(core * kv_rows, kv_rows), kv_rows)

    def kv_out(k):
        target = lax.rem(me_h + k, n_head)
        return remote(
            kvw.at[target, kv_half], kvr.at[me_h, kv_half], kv_sems.at[k - 1], target, "heads"
        )

    def kv_in(k):
        ref = kvr.at[lax.rem(me_h - k + n_head, n_head), kv_half]
        return remote(ref, ref, kv_sems.at[k - 1], lax.rem(me_h + k, n_head), "heads")

    order = sorted(range(1, n_head), key=lambda k: min(k, n_head - k))
    for k in order:
        kv_out(k).start()

    own_copies = [
        pltpu.make_async_copy(own_w, whole_w.at[me], local_sems.at[5]),
        pltpu.make_async_copy(own_kv, win.at[0], local_sems.at[1]),
        pltpu.make_async_copy(kvw.at[me_h], kvr.at[me_h], local_sems.at[2]),
    ]
    for copy in own_copies:
        copy.start()

    own_copies[1].wait()
    cache_in.wait()
    size = cache_rows // 4
    parts = cache_v.shape[0] // size

    def split(k):
        spread[0:size, :] = cache_v[k * size : (k + 1) * size, :].astype(jnp.float32)
        at = slice(k * size // 2, (k + 1) * size // 2)
        keys[at, :] = spread[pl.ds(0, size // 2, stride=2), :].astype(jnp.bfloat16)
        values[at, :] = spread[pl.ds(1, size // 2, stride=2), :].astype(jnp.bfloat16)

    def split_window(b):
        spread[0 : 2 * tokens, :] = win[b].astype(f32)
        win_k[b] = spread[pl.ds(0, tokens, stride=2), :].astype(bf16)
        win_v[b] = spread[pl.ds(1, tokens, stride=2), :].astype(bf16)

    def attend_window(g):
        cols = slice(g * DH, (g + 1) * DH)
        q = query_ref[:, cols]
        count = q.shape[0]
        acc = jnp.zeros((count, 2 * DH), jnp.float32)
        top = jnp.full((count, 1), -1e30, jnp.float32)
        row = lax.broadcasted_iota(jnp.int32, (count, count), 0)
        col = lax.broadcasted_iota(jnp.int32, (count, count), 1)
        ones = jnp.ones((count, DH), jnp.bfloat16)
        reach = win.shape[0]
        for b in range(reach):
            s = lax.dot_general(
                q, win_k[b], (((1,), (1,)), ((), ())), preferred_element_type=jnp.float32
            )
            if b == 0:
                s = jnp.where(col <= row, s, -1e30)
            else:
                s = s + jnp.where(me >= b, jnp.float32(0.0), jnp.float32(-1e30))
            if b == reach - 1:
                s = jnp.where(col > row, s, -1e30)
            here = jnp.maximum(top, jnp.max(s, axis=1, keepdims=True))
            p = jnp.exp2((s - here) * SCALE2).astype(jnp.bfloat16)
            shrink = jnp.exp2((top - here) * SCALE2)
            both = jnp.concatenate([win_v[b], ones], axis=1)
            acc = acc * shrink + jnp.dot(p, both, preferred_element_type=jnp.float32)
            top = here
        att[:, cols] = (acc[:, :DH] / acc[:, DH:]).astype(jnp.bfloat16)

    def soft(q, acc, top, keys_b, values_b, bias_b):
        s = lax.dot_general(q, keys_b, (((1,), (1,)), ((), ())), preferred_element_type=f32)
        if bias_b is not None:
            s = s + bias_b
        here = jnp.maximum(top, jnp.max(s, axis=1, keepdims=True))
        p = jnp.exp2((s - here) * SCALE2).astype(bf16)
        shrink = jnp.exp2((top - here) * SCALE2)
        both = jnp.concatenate([values_b, jnp.ones_like(values_b)], axis=1)
        return acc * shrink + jnp.dot(p, both, preferred_element_type=f32), here

    def head_of(held, g):
        at = pl.multiple_of(g * DH, DH)
        return held[:, :, pl.ds(at, DH)].astype(f32).reshape(-1, DH).astype(bf16)

    def soft_old(q):
        acc = jnp.zeros((q.shape[0], 2 * DH), f32)
        top = jnp.full((q.shape[0], 1), -1e30, f32)
        for b in range(cache_rows // block):
            at = slice(b * block, (b + 1) * block)
            acc, top = soft(q, acc, top, keys[at, :], values[at, :], bias[:, at])
        return acc, top

    heads_here = width // DH
    third = -(-heads_here // 3)
    old_spans = {-1: (0, third), 1: (third, 2 * third), 2: (2 * third, heads_here)}
    early = [functools.partial(split, k) for k in range(parts)]
    late = [functools.partial(attend_window, g) for g in range(query_ref.shape[1] // DH)]

    def fill(work, amount=1):
        for _ in range(amount):
            if work:
                work.pop(0)()

    win_in = lambda b, k: remote(win.at[b], win.at[b], win_sems.at[k], partner)

    def relay(src, dst, k):
        return remote(win.at[src], win.at[dst], win_sems.at[k], partner)

    for name in ("a+", "a-"):
        way = 1 if name[1] == "+" else -1
        for half in halves:
            first_in(half, name).wait_recv()
            first(half, "f" + name[1]).start()
            for other in ("a+", "a-"):
                second(half, -way, other).start()
            share(half, -way, 0)
        fill(early)
    q0_held[me] = sum_query(0)
    gather_start(q0_held, tok_sems.at[2, 1], *tok)
    win_in(2, 0).wait_recv()
    relay(2 * core, 1, 2).start()
    for name in ("a+", "a-"):
        way = 1 if name[1] == "+" else -1
        for half in halves:
            second_in(half, 0, name).wait_recv()
            second(half, 0, "f" + name[1]).start()
            share(half, 0, -way)
        fill(early)
    for half in halves:
        first_in(half, "f+").wait_recv()
        first_in(half, "f-").wait_recv()
        for other in ("a+", "a-"):
            second(half, 2, other).start()
        share(half, 2, 0)
    win_in(4, 1).wait_recv()
    relay(2 + 2 * core, 3, 3).start()
    for i in (-1, 1):
        for name in ("a+", "a-"):
            way = 1 if name[1] == "+" else -1
            for half in halves:
                second_in(half, i, name).wait_recv()
                second(half, i, "f" + name[1]).start()
                share(half, i, -way)
            fill(early)
    fill(early, parts)
    win_in(1, 2).wait_recv()
    win_in(3, 3).wait_recv()
    for b in range(win.shape[0]):
        split_window(b)
    def kv_share(k):
        ref = kvr.at[lax.rem(me_h - k + n_head, n_head), kv_half]
        return remote(ref, ref, kv_pair_sems.at[k - 1], partner)

    def kv_share_in(k):
        other = pl.ds(pl.multiple_of((1 - core) * kv_rows, kv_rows), kv_rows)
        ref = kvr.at[lax.rem(me_h - k + n_head, n_head), other]
        return remote(ref, ref, kv_pair_sems.at[k - 1], partner)

    fill(late)
    for half in halves:
        second_in(half, 0, "f+").wait_recv()
        second_in(half, 0, "f-").wait_recv()
        share(half, 0, 2)
    for name in ("a+", "a-"):
        way = 1 if name[1] == "+" else -1
        for half in halves:
            second_in(half, 2, name).wait_recv()
            second(half, 2, "f" + name[1]).start()
            share(half, 2, -way)
        fill(late)
    for i in (-1, 1, 2):
        for half in halves:
            second_in(half, i, "f+").wait_recv()
            second_in(half, i, "f-").wait_recv()
            share(half, i, 2)
        if i == -1:
            fill(late, len(late))
            finish(q0_held, tok_sems.at[2, 1], *tok)
        low, high = old_spans[i]

        def old_head(g, carry):
            acc, top = soft_old(head_of(q0_held, g))
            acc_s[g] = acc
            top_s[g] = jnp.broadcast_to(top, (beams, DH))
            return carry

        lax.fori_loop(low, high, old_head, 0)
    half_of_all = whole_w.at[pl.ds(0, n_tok // 2)]
    pair_all = remote(half_of_all, half_of_all, pair_sems, partner)
    pair_all.wait_recv()
    own_copies[0].wait()

    heads_here = width // DH
    half_rows = tokens // 2
    middle = n_head // 2
    rows_sub = half_rows // subs
    rows_sub2 = tokens // subs2
    wrap = lambda value: lax.rem(value + 2 * n_head, n_head)
    lanes = [(sub, way) for sub in range(subs) for way in (0, 1)]
    sign = (1, -1)
    at_rows = lambda sub, way: slice(way * half_rows + sub * rows_sub, way * half_rows + (sub + 1) * rows_sub)

    def product(c):
        per = n_tok // n_head
        w = whole_w[pl.ds(c * per, per)].reshape(width, width)
        part[c] = lax.dot_general(
            att[...], w, (((1,), (1,)), ((), ())), preferred_element_type=f32
        )

    def sum_copy(step, sub, way):
        return pltpu.make_async_remote_copy(
            src_ref=s_buf.at[step, way, sub],
            dst_ref=r_buf.at[step, way, sub],
            send_sem=s_sems.at[step, way, sub],
            recv_sem=r_sems.at[step, way, sub],
            device_id={"heads": wrap(me_h + sign[way])},
            device_id_type=MESH,
        )

    def spread_kv(c):
        count = width
        spread[0 : 2 * count, :] = kvr[c].astype(f32)
        kvd[c, :, :DH] = spread[pl.ds(0, count, stride=2), :].astype(bf16)
        kvd[c, :, DH:] = spread[pl.ds(1, count, stride=2), :].astype(bf16)

    product(wrap(me_h - 1))
    product(wrap(me_h + 1))

    def work(step, slot):
        if slot < 2:

            @pl.when(step < middle - 1)
            def _():
                if slot == 0:
                    product(wrap(me_h - 2 - step))
                else:
                    product(lax.select(step == middle - 2, me_h, wrap(me_h + 2 + step)))

            @pl.when(step >= n_head - 3)
            def _():
                spread_kv((step - (n_head - 3)) * 4 + slot * 2)
                spread_kv((step - (n_head - 3)) * 4 + slot * 2 + 1)

    def reduce_step(step, carry):
        for sub in range(subs):
            for way in (0, 1):
                c = wrap(me_h - sign[way] * (1 + step))
                own = part[c, at_rows(sub, way), :]

                @pl.when(step == 0)
                def _():
                    s_buf[step, way, sub] = own.astype(bf16)

                @pl.when(step > 0)
                def _():
                    sum_copy(step - 1, sub, way).wait_recv()
                    s_buf[step, way, sub] = (
                        own + r_buf[step - 1, way, sub].astype(f32)
                    ).astype(bf16)

                sum_copy(step, sub, way).start()
            if sub == 0:

                @pl.when(step == n_head - 3)
                def _():
                    for k in order:
                        kv_share_in(k).wait_recv()
                    own_copies[2].wait()

            for slot in range(sub * 2 // subs, (sub + 1) * 2 // subs):
                work(step, slot)

        @pl.when(step == middle - 1)
        def _():
            for k in order:
                kv_in(k).wait_recv()
                kv_share(k).start()

        return carry

    lax.fori_loop(0, n_head - 1, reduce_step, 0)

    last = n_head - 2
    for sub, way in lanes:
        rows = at_rows(sub, way)
        sum_copy(last, sub, way).wait_recv()
        total = part[me_h, rows, :] + r_buf[last, way, sub].astype(f32)
        hid_out_ref[rows, :] = (hid_ref[rows, :].astype(f32) + total).astype(bf16)

    hid_out = pltpu.make_async_copy(hid_out_ref, hid_out_hbm, local_sems.at[0])
    hid_out.start()

    hidden = hid_out_ref[...].astype(f32)
    scaled = (hidden * gain_ref[...].astype(f32)).astype(bf16)

    def product2(c):
        part2[c] = jnp.dot(scaled, kvd[c], preferred_element_type=f32)

    count = (middle, n_head - 1 - middle)

    def chunk(step, way):
        return wrap(me_h + middle - step) if way == 0 else wrap(me_h - count[1] + step)

    def share_copy(step, sub, way):
        return pltpu.make_async_remote_copy(
            src_ref=s_buf2.at[step, way, sub],
            dst_ref=r_buf2.at[step, way, sub],
            send_sem=s_sems2.at[step, way, sub],
            recv_sem=r_sems2.at[step, way, sub],
            device_id={"heads": wrap(me_h + sign[way])},
            device_id_type=MESH,
        )

    product2(chunk(0, 0))
    product2(chunk(0, 1))
    for step in range(middle):
        for sub in range(subs2):
            rows = slice(sub * rows_sub2, (sub + 1) * rows_sub2)
            for way in (0, 1):
                if step >= count[way]:
                    continue
                value = part2[chunk(step, way), rows, :]
                if step:
                    share_copy(step - 1, sub, way).wait_recv()
                    value = value + r_buf2[step - 1, way, sub].astype(f32)
                s_buf2[step, way, sub] = value.astype(bf16)
                share_copy(step, sub, way).start()
        if step == 0:
            flat = (hidden * hidden).astype(bf16)
            ones = jnp.ones((8, width), bf16)
            squares[me_h] = lax.dot_general(
                ones, flat, (((1,), (1,)), ((), ())), preferred_element_type=f32
            )
            gather_start(squares, sq_sems, *head)
        for way in (0, 1):
            if step + 1 < count[way]:
                product2(chunk(step + 1, way))
        if step == middle - 1:
            product2(me_h)
    finish(squares, sq_sems, *head)
    mean = jnp.transpose(jnp.sum(squares[...], axis=0))[:, :1] / D
    factor = lax.rsqrt(mean + EPSILON)
    for sub in range(subs2):
        rows = slice(sub * rows_sub2, (sub + 1) * rows_sub2)
        total = part2[me_h, rows, :]
        for way in (0, 1):
            share_copy(count[way] - 1, sub, way).wait_recv()
            total = total + r_buf2[count[way] - 1, way, sub].astype(f32)
        fresh = total * factor[rows]
        fk[rows, :] = fresh[:, :DH].astype(bf16)
        fv[rows, :] = fresh[:, DH:].astype(bf16)

    lane8 = lax.broadcasted_iota(jnp.int32, (tokens, DH), 1)
    sends = (oa_send, ob_send)
    spans = ((0, split_at), (split_at, heads_here))

    def put_head(layer, group, g, acc, top):
        amount = acc[:, DH:]
        out = (acc[:, :DH] / amount).reshape(n_tok, -1, DH).astype(bf16)
        at = pl.multiple_of((g - spans[group][0]) * DH, DH)
        sends[group][layer, :, :, pl.ds(at, DH)] = out
        value = top * SCALE2 + jnp.log2(amount)
        mine = (lane8 % 8 == g) & (lane8 < 24)
        lse_s[...] = jnp.where(mine, value, lse_s[...])

    def send_group(layer, group):
        value = lse_s[...]
        high = value.astype(bf16).astype(f32)
        mid = (value - high).astype(bf16).astype(f32)
        low = value - high - mid
        packed = jnp.where(lane8 < 8, high, jnp.where(lane8 < 16, mid, low))
        wide = (spans[group][1] - spans[group][0]) * DH
        sends[group][layer, :, :, wide:] = packed.reshape(n_tok, -1, DH).astype(bf16)
        recv = (oa_recv, ob_recv)[group].at[layer]
        scatter_start(sends[group].at[layer], recv, tok_sems.at[layer, group], *tok)

    def mix_group(layer, group):
        recv = (oa_recv, ob_recv)[group].at[layer]
        held = (oa_held, ob_held)[group].at[layer]
        low, high = spans[group]
        wide = (high - low) * DH
        recv[me] = sends[group][layer, me]
        finish(recv, tok_sems.at[layer, group], *tok)
        packed = recv[:, :, wide:].astype(f32)
        lse = (
            packed[:, :, low:high]
            + packed[:, :, 8 + low : 8 + high]
            + packed[:, :, 16 + low : 16 + high]
        )
        weight = jnp.exp2(lse - jnp.max(lse, axis=0, keepdims=True))
        share = weight / jnp.sum(weight, axis=0, keepdims=True)
        for k in range(high - low):
            cols = slice(k * DH, (k + 1) * DH)
            mixed = jnp.sum(recv[:, :, cols].astype(f32) * share[:, :, k : k + 1], axis=0)
            held[me, :, cols] = mixed.astype(bf16)
        gather_start(held, tok_sems.at[layer, 2 + group], *tok)

    def branch_of(layer, group):
        held = (oa_held, ob_held)[group].at[layer]
        finish(held, tok_sems.at[layer, 2 + group], *tok)
        low, high = spans[group]
        wide = (high - low) * DH
        whole = held[...].astype(f32).reshape(-1, wide).astype(bf16)
        return both_of(whole, wo.at[:, :, pl.ds(low * DH, wide)], layer)

    def project(layer, before):
        mix_group(layer, 0)
        mix_group(layer, 1)
        one, two = branch_of(layer, 0), branch_of(layer, 1)
        send, recv, held = b_send.at[layer], b_recv.at[layer], s_held.at[layer]
        pack(send, one[0] + two[0], one[1] + two[1])
        scatter_start(send, recv, head_sems.at[layer, 0], *head)
        recv[me_h] = send[me_h]
        finish(recv, head_sems.at[layer, 0], *head)
        total = jnp.sum(recv[...].astype(f32), axis=0)
        held[me_h] = (before[me_h].astype(f32) + total).astype(bf16)
        gather_start(held, head_sems.at[layer, 1], *head)
        finish(held, head_sems.at[layer, 1], *head)

    lse_s[...] = jnp.zeros(lse_s.shape, f32)
    for group in (0, 1):
        for g in range(*spans[group]):
            acc, top = soft(head_of(q0_held, g), acc_s[g], top_s[g][:, :1], fk[...], fv[...], None)
            put_head(0, group, g, acc, top)
        send_group(0, group)

    spread[pl.ds(0, tokens, stride=2), :] = fk[...].astype(f32)
    spread[pl.ds(1, tokens, stride=2), :] = fv[...].astype(f32)
    pages[0:own_pages] = spread[0 : 2 * tokens, :].reshape(own_pages, -1, DH).astype(bf16)
    pages[own_pages:] = jnp.zeros((n_tok - own_pages, *pages.shape[1:]), bf16)
    shift = lax.div(home_ref[0], pages_here)

    def stage(peer, carry):
        which = lax.rem(peer - shift - own_pages * me + 2 * n_tok * own_pages, n_tok)
        outbox[peer] = pages[which]
        return carry

    lax.fori_loop(0, n_tok, stage, 0)
    scatter_start(outbox, inbox, page_sems, *tok)
    inbox[me] = outbox[me]

    wo_in.wait()
    project(0, state_ref)
    send_query(1, unpack(s_held[0].astype(f32)))()
    ready = sum_query(1)
    cut = split_at * DH
    qa_held[me] = ready[:, :cut]
    gather_start(qa_held, tok_sems.at[3, 1], *tok)
    qb_held[me] = ready[:, cut:]
    gather_start(qb_held, tok_sems.at[3, 2], *tok)
    for group, held in ((0, qa_held), (1, qb_held)):
        finish(held, tok_sems.at[3, 1 + group], *tok)

        def one_head(g, carry, group=group, held=held):
            q = head_of(held, g - spans[group][0])
            acc, top = soft_old(q)
            acc, top = soft(q, acc, top, fk[...], fv[...], None)
            put_head(1, group, g, acc, top)
            return carry

        lax.fori_loop(*spans[group], one_head, 0)
        send_group(1, group)
    finish(inbox, page_sems, *tok)
    inbox_out = pltpu.make_async_copy(inbox, inbox_hbm, local_sems.at[1])
    inbox_out.start()
    project(1, s_held.at[0])
    ended = jnp.transpose(jnp.concatenate(unpack(s_held[1].astype(f32)), axis=1))
    state_end[...] = ended[:cols].astype(bf16)
    state_out = pltpu.make_async_copy(state_end, state_out_hbm, local_sems.at[2])
    state_out.start()
    hid_out.wait()
    inbox_out.wait()
    state_out.wait()

    def drain(step, carry):
        for sub, way in lanes:
            sum_copy(step, sub, way).wait_send()
        return carry

    lax.fori_loop(0, n_head - 1, drain, 0)
    for way in (0, 1):
        for step in range(count[way]):
            for sub in range(subs2):
                share_copy(step, sub, way).wait_send()
    relay(2 * core, 1, 2).wait_send()
    relay(2 + 2 * core, 3, 3).wait_send()
    win_two.wait_send()
    win_four.wait_send()
    for half in halves:
        for name in ("a+", "a-", "f+", "f-"):
            first(half, name).wait_send()
            for i in (0, -1, 1, 2):
                second(half, i, name).wait_send()
    for k in order:
        kv_out(k).wait_send()
        kv_share(k).wait_send()
    pair_all.wait_send()


def whole(
    n_tok,
    n_head,
    page_home,
    cache_len,
    parents,
    queries,
    hidden,
    gain,
    beams_t,
    beam_gain,
    own_w,
    own_kv,
    kvw,
    cache,
    wo,
    wq,
    side=4,
    subs=4,
    subs2=2,
    block=512,
):
    tokens, width = hidden.shape
    cols, beams = beams_t.shape
    bf16, f32 = jnp.bfloat16, jnp.float32
    heads_here = width // DH
    split_at = (heads_here + 1) // 2
    wide_a, wide_b = split_at * DH, (heads_here - split_at) * DH
    rows = beams // n_tok
    reach = WINDOW // tokens + 1
    cache_rows = cache.shape[0] // 2
    state3 = (n_head, beams // n_head * cols // DH, DH)
    pieces = (2, subs, tokens // 2 // subs, width)
    pieces2 = (2, subs2, tokens // subs2, 2 * DH)
    box = (n_tok, 2 * PAGE, DH)
    hbm = pl.BlockSpec(memory_space=pltpu.HBM)
    vmem, dma = pltpu.VMEM, pltpu.SemaphoreType.DMA
    return pl.pallas_call(
        functools.partial(whole_kernel, n_tok, n_head, side, subs, subs2, block, split_at),
        out_shape=[
            jax.ShapeDtypeStruct(hidden.shape, bf16),
            jax.ShapeDtypeStruct(box, bf16),
            jax.ShapeDtypeStruct(beams_t.shape, bf16),
        ],
        in_specs=[hbm] * 14,
        out_specs=[hbm] * 3,
        scratch_shapes=[
            vmem(beams_t.shape, bf16),
            vmem(hidden.shape, bf16),
            pltpu.SMEM(page_home.shape, jnp.int32),
            pltpu.SMEM(cache_len.shape, jnp.int32),
            vmem((1, beams), jnp.int32),
            vmem(queries.shape, bf16),
            vmem(hidden.shape, bf16),
            vmem((1, width), bf16),
            vmem((2 * DH, beams), bf16),
            vmem(beam_gain.shape, bf16),
            vmem((n_tok, *own_w.shape), bf16),
            vmem((reach, *own_kv.shape), bf16),
            vmem((reach, tokens, DH), bf16),
            vmem((reach, tokens, DH), bf16),
            vmem((tokens, width), bf16),
            vmem(state3, bf16),
            vmem(cache.shape, bf16),
            vmem((n_head, tokens, width), f32),
            vmem((n_head - 1, *pieces), bf16),
            vmem((n_head - 1, *pieces), bf16),
            vmem((n_head, tokens, 2 * DH), f32),
            vmem((n_head // 2, *pieces2), bf16),
            vmem((n_head // 2, *pieces2), bf16),
            vmem((n_head, 8, tokens), f32),
            vmem(kvw.shape, bf16),
            vmem((n_head, width, 2 * DH), bf16),
            vmem((2 * width, DH), f32),
            vmem((cache_rows, DH), bf16),
            vmem((cache_rows, DH), bf16),
            vmem((LAYERS, 2 * DH, width), bf16),
            vmem(wq.shape, bf16),
            vmem((1, cache_rows), f32),
            vmem((heads_here, beams, 2 * DH), f32),
            vmem((heads_here, beams, DH), f32),
            vmem((tokens, DH), bf16),
            vmem((tokens, DH), bf16),
            vmem(box, bf16),
            vmem(box, bf16),
            vmem(box, bf16),
            vmem((beams, DH), f32),
            vmem((LAYERS, n_tok, rows, wide_a + DH), bf16),
            vmem((LAYERS, n_tok, rows, wide_b + DH), bf16),
            vmem((LAYERS, n_tok, rows, wide_a + DH), bf16),
            vmem((LAYERS, n_tok, rows, wide_b + DH), bf16),
            vmem((LAYERS, n_tok, rows, wide_a), bf16),
            vmem((LAYERS, n_tok, rows, wide_b), bf16),
            vmem((LAYERS, *state3), bf16),
            vmem((LAYERS, *state3), bf16),
            vmem((LAYERS, *state3), bf16),
            vmem((LAYERS, n_tok, rows, width + DH), bf16),
            vmem((LAYERS, n_tok, rows, width + DH), bf16),
            vmem((n_tok, rows, wide_a), bf16),
            vmem((n_tok, rows, wide_b), bf16),
            vmem((n_tok, rows, width), bf16),
            dma((6,)),
            dma((8,)),
            dma((40, 2)),
            dma((2,)),
            dma((4, 2)),
            dma((n_head - 1, 2)),
            dma((n_head - 1, 2)),
            dma((n_head - 1, 2, subs)),
            dma((n_head - 1, 2, subs)),
            dma((n_head // 2, 2, subs2)),
            dma((n_head // 2, 2, subs2)),
            dma((2,)),
            dma((2,)),
            dma((LAYERS + 2, 4, 2)),
            dma((LAYERS, 2, 2)),
        ],
        compiler_params=pltpu.CompilerParams(
            collective_id=1, has_side_effects=True, vmem_limit_bytes=67000000
        ),
        name="whole",
    )(
        page_home,
        cache_len,
        parents[None, :],
        queries,
        hidden,
        gain[None, :],
        beams_t,
        beam_gain,
        own_w,
        own_kv,
        kvw,
        cache,
        wo,
        wq,
    )


def place_kernel(
    n_tok,
    own_pages,
    home_ref,
    cache_hbm,
    inbox_hbm,
    hid_hbm,
    state_hbm,
    out_ref,
    hid_out,
    state_out,
    cache,
    inbox,
    hid,
    state,
    sems,
):
    me = lax.axis_index("tokens")
    rows = inbox.shape[1]
    pages_here = out_ref.shape[0] // rows
    size = cache.shape[0] // 4
    parts = [pl.ds(k * size, size) for k in range(4)]
    loads = [
        pltpu.make_async_copy(cache_hbm.at[at], cache.at[at], sems.at[0, k])
        for k, at in enumerate(parts)
    ]
    stores = [
        pltpu.make_async_copy(cache.at[at], out_ref.at[at], sems.at[1, k])
        for k, at in enumerate(parts)
    ]
    for load in loads:
        load.start()
    hid_in = pltpu.make_async_copy(hid_hbm, hid, sems.at[2, 0])
    inbox_in = pltpu.make_async_copy(inbox_hbm, inbox, sems.at[2, 1])
    hid_store = pltpu.make_async_copy(hid, hid_out, sems.at[2, 2])
    state_in = pltpu.make_async_copy(state_hbm, state, sems.at[3, 0])
    state_store = pltpu.make_async_copy(state, state_out, sems.at[3, 1])
    inbox_in.start()
    hid_in.start()
    state_in.start()
    for load, store in zip(loads, stores):
        load.wait()
        store.start()
    hid_in.wait()
    hid_store.start()
    state_in.wait()
    state_store.start()
    inbox_in.wait()
    for store in stores:
        store.wait()

    def each(act):
        def one(slot, carry):
            page = page_slot(home_ref, me, own_pages, pages_here, n_tok, slot)

            @pl.when(page >= 0)
            def _():
                at = pl.ds(pl.multiple_of(page * rows, rows), rows)
                act(pltpu.make_async_copy(inbox.at[slot], out_ref.at[at], sems.at[2, 3]))

            return carry

        lax.fori_loop(0, n_tok, one, 0)

    each(lambda copy: copy.start())
    each(lambda copy: copy.wait())
    hid_store.wait()
    state_store.wait()


def place_pages(n_tok, own_pages, page_home, cache, inbox, hidden, state):
    hbm = pl.BlockSpec(memory_space=pltpu.HBM)
    return pl.pallas_call(
        functools.partial(place_kernel, n_tok, own_pages),
        out_shape=[
            jax.ShapeDtypeStruct(cache.shape, cache.dtype),
            jax.ShapeDtypeStruct(hidden.shape, hidden.dtype),
            jax.ShapeDtypeStruct(state.shape, state.dtype),
        ],
        in_specs=[pl.BlockSpec(memory_space=pltpu.SMEM)] + [hbm] * 4,
        out_specs=[hbm] * 3,
        scratch_shapes=[
            pltpu.VMEM(cache.shape, cache.dtype),
            pltpu.VMEM(inbox.shape, inbox.dtype),
            pltpu.VMEM(hidden.shape, hidden.dtype),
            pltpu.VMEM(state.shape, state.dtype),
            pltpu.SemaphoreType.DMA((4, 4)),
        ],
        compiler_params=pltpu.CompilerParams(vmem_limit_bytes=67000000),
        name="place_pages",
    )(page_home, cache, inbox, hidden, state)


def shards(
    hidden_in,
    queries,
    keyvals,
    out_weight,
    kv_gain,
    kv_weight,
    cache,
    page_home,
    cache_len,
    beam_state,
    parents,
    beam_gain,
    query_weight,
    beam_out_weight,
):
    n_tok = lax.axis_size("tokens")
    n_head = lax.axis_size("heads")
    flat_cache = cache.reshape(-1, DH)
    hidden, inbox, beams_end = whole(
        n_tok,
        n_head,
        page_home,
        cache_len,
        parents,
        queries,
        hidden_in,
        kv_gain,
        beam_state.T,
        beam_gain,
        out_weight.T,
        keyvals.reshape(-1, DH),
        kv_weight.reshape(n_head, -1, DH),
        flat_cache,
        jnp.swapaxes(beam_out_weight, 1, 2),
        query_weight,
    )
    own_pages = hidden_in.shape[0] // PAGE
    new_cache, stretch_hidden, beams_end = place_pages(
        n_tok, own_pages, page_home, flat_cache, inbox, hidden, beams_end
    )
    return (stretch_hidden, new_cache.reshape(cache.shape), beams_end.T)


def solution(mesh):
    tokens = "tokens"
    placed = (
        P(tokens, "heads"),
        P(tokens, "heads"),
        P(tokens, None, "heads"),
        P("heads", tokens),
        P("heads"),
        P(None, None, "heads"),
        P(tokens, None, "heads"),
        P(),
        P(),
        P(None, tokens),
        P(),
        P(None, tokens),
        P(None, tokens, "heads"),
        P(None, "heads", tokens),
    )
    return jax.shard_map(
        shards,
        mesh=mesh,
        in_specs=placed,
        out_specs=(P(tokens, "heads"), P(tokens, None, "heads"), P(None, tokens)),
        check_vma=False,
    )
```

profile of v0, /device:TPU:1, one launch (start us, length us, event | category | flops | bytes accessed | tf_op | source)
XLA Modules:
  0.0 178.4 jit_solution(6065748198856341282)
XLA Ops:
  1.3 1.3 broadcast_in_dim.7.gain_hbm
  2.5 171.5 %whole.1 = (bf16[256,640]{1,0:T(8,128)(2,1)}, bf16[32,32,128]{2,1,0:T(8,128)(2,1)}, bf16[160,256]{1,0:T(8,128)(2,1)}) custom-call(s32[512]{0:T(512)} %home_ref.1, s32[1]{0:T(128)S(6)} %copy.17.len_hbm, s32[1,256]{1,0:T(1,128)} %bitcast.16, bf16[256,640]{1,0:T(8,128)(2,1)} %query_hbm.1, bf16[256,640]{1,0:T(8,128)(2,1)} %hid_hbm.1, ...), custom_call_target="tpu_custom_call" | custom-call | tf_op jit(solution)/shard_map/whole/pallas_call | solution.py:937
  174.1 4.1 %place_pages.1 = (bf16[8192,128]{1,0:T(8,128)(2,1)}, bf16[256,640]{1,0:T(8,128)(2,1)}, bf16[160,256]{1,0:T(8,128)(2,1)}) custom-call(s32[512]{0:T(512)} %home_ref.1, bf16[8192,128]{1,0:T(8,128)(2,1)} %bitcast.10, bf16[32,32,128]{2,1,0:T(8,128)(2,1)} %get-tuple-element.9.inbox_hbm, bf16[256,640]{1,0:T(8,128)(2,1)} %get-tuple-element.10.hid_hbm, ...), custom_call_target="tpu_custom_call" | custom-call | tf_op jit(solution)/shard_map/place_pages/pallas_call | solution.py:1111
where the time goes:
time: 179 us; the launch traced here: 178 us
  Pallas kernels  176 us (98%)
    pallas_call x1, Pallas kernels, whole(): pl.pallas_call(functools.partial(whole_kernel, n_tok, n_head, side, subs,...  172 us
    pallas_call x1, Pallas kernels, place_pages(): pl.pallas_call(functools.partial(place_kernel, n_tok, own_pages), out_sha...  4.12 us

commit v1 on v0

--- a/solution.py
+++ b/solution.py
@@ -307,7 +307,6 @@
     bias[...] = jnp.where(kept, 0.0, -1e30).astype(f32)
 
     pl.semaphore_wait(pltpu.get_barrier_semaphore(), n_tok + n_head - 2)
-    start_query()
 
     def remote(src, dst, sems, target, axis="tokens"):
         return pltpu.make_async_remote_copy(
@@ -468,31 +467,6 @@
             top = here
         att[:, cols] = (acc[:, :DH] / acc[:, DH:]).astype(jnp.bfloat16)
 
-    def soft(q, acc, top, keys_b, values_b, bias_b):
-        s = lax.dot_general(q, keys_b, (((1,), (1,)), ((), ())), preferred_element_type=f32)
-        if bias_b is not None:
-            s = s + bias_b
-        here = jnp.maximum(top, jnp.max(s, axis=1, keepdims=True))
-        p = jnp.exp2((s - here) * SCALE2).astype(bf16)
-        shrink = jnp.exp2((top - here) * SCALE2)
-        both = jnp.concatenate([values_b, jnp.ones_like(values_b)], axis=1)
-        return acc * shrink + jnp.dot(p, both, preferred_element_type=f32), here
-
-    def head_of(held, g):
-        at = pl.multiple_of(g * DH, DH)
-        return held[:, :, pl.ds(at, DH)].astype(f32).reshape(-1, DH).astype(bf16)
-
-    def soft_old(q):
-        acc = jnp.zeros((q.shape[0], 2 * DH), f32)
-        top = jnp.full((q.shape[0], 1), -1e30, f32)
-        for b in range(cache_rows // block):
-            at = slice(b * block, (b + 1) * block)
-            acc, top = soft(q, acc, top, keys[at, :], values[at, :], bias[:, at])
-        return acc, top
-
-    heads_here = width // DH
-    third = -(-heads_here // 3)
-    old_spans = {-1: (0, third), 1: (third, 2 * third), 2: (2 * third, heads_here)}
     early = [functools.partial(split, k) for k in range(parts)]
     late = [functools.partial(attend_window, g) for g in range(query_ref.shape[1] // DH)]
 
@@ -515,8 +489,6 @@
                 second(half, -way, other).start()
             share(half, -way, 0)
         fill(early)
-    q0_held[me] = sum_query(0)
-    gather_start(q0_held, tok_sems.at[2, 1], *tok)
     win_in(2, 0).wait_recv()
     relay(2 * core, 1, 2).start()
     for name in ("a+", "a-"):
@@ -573,18 +545,9 @@
             second_in(half, i, "f+").wait_recv()
             second_in(half, i, "f-").wait_recv()
             share(half, i, 2)
-        if i == -1:
-            fill(late, len(late))
-            finish(q0_held, tok_sems.at[2, 1], *tok)
-        low, high = old_spans[i]
-
-        def old_head(g, carry):
-            acc, top = soft_old(head_of(q0_held, g))
-            acc_s[g] = acc
-            top_s[g] = jnp.broadcast_to(top, (beams, DH))
-            return carry
-
-        lax.fori_loop(low, high, old_head, 0)
+        if i != 2:
+            fill(late)
+    fill(late, len(late))
     half_of_all = whole_w.at[pl.ds(0, n_tok // 2)]
     pair_all = remote(half_of_all, half_of_all, pair_sems, partner)
     pair_all.wait_recv()
@@ -617,14 +580,53 @@
             device_id_type=MESH,
         )
 
+    def soft(q, acc, top, keys_b, values_b, bias_b):
+        s = lax.dot_general(q, keys_b, (((1,), (1,)), ((), ())), preferred_element_type=f32)
+        if bias_b is not None:
+            s = s + bias_b
+        here = jnp.maximum(top, jnp.max(s, axis=1, keepdims=True))
+        p = jnp.exp2((s - here) * SCALE2).astype(bf16)
+        shrink = jnp.exp2((top - here) * SCALE2)
+        both = jnp.concatenate([values_b, jnp.ones_like(values_b)], axis=1)
+        return acc * shrink + jnp.dot(p, both, preferred_element_type=f32), here
+
+    def head_of(held, g):
+        at = pl.multiple_of(g * DH, DH)
+        return held[:, :, pl.ds(at, DH)].astype(f32).reshape(-1, DH).astype(bf16)
+
+    def soft_old(q):
+        acc = jnp.zeros((q.shape[0], 2 * DH), f32)
+        top = jnp.full((q.shape[0], 1), -1e30, f32)
+        for b in range(cache_rows // block):
+            at = slice(b * block, (b + 1) * block)
+            acc, top = soft(q, acc, top, keys[at, :], values[at, :], bias[:, at])
+        return acc, top
+
     def spread_kv(c):
         count = width
         spread[0 : 2 * count, :] = kvr[c].astype(f32)
         kvd[c, :, :DH] = spread[pl.ds(0, count, stride=2), :].astype(bf16)
         kvd[c, :, DH:] = spread[pl.ds(1, count, stride=2), :].astype(bf16)
 
+    start_query()
     product(wrap(me_h - 1))
     product(wrap(me_h + 1))
+
+    begin_old = middle
+
+    def old_half(g, k):
+        q = head_of(q0_held, g)
+        if k == 0:
+            acc = jnp.zeros((beams, 2 * DH), f32)
+            top = jnp.full((beams, 1), -1e30, f32)
+        else:
+            acc, top = acc_s[g], top_s[g][:, :1]
+        per = cache_rows // block // 2
+        for b in range(k * per, (k + 1) * per):
+            where = slice(b * block, (b + 1) * block)
+            acc, top = soft(q, acc, top, keys[where, :], values[where, :], bias[:, where])
+        acc_s[g] = acc
+        top_s[g] = jnp.broadcast_to(top, (beams, DH))
 
     def work(step, slot):
         if slot < 2:
@@ -641,6 +643,12 @@
                 spread_kv((step - (n_head - 3)) * 4 + slot * 2)
                 spread_kv((step - (n_head - 3)) * 4 + slot * 2 + 1)
 
+        else:
+
+            @pl.when(step >= begin_old)
+            def _():
+                old_half(jnp.maximum(step - begin_old, 0), slot - 2)
+
     def reduce_step(step, carry):
         for sub in range(subs):
             for way in (0, 1):
@@ -667,7 +675,7 @@
                         kv_share_in(k).wait_recv()
                     own_copies[2].wait()
 
-            for slot in range(sub * 2 // subs, (sub + 1) * 2 // subs):
+            for slot in range(sub * 4 // subs, (sub + 1) * 4 // subs):
                 work(step, slot)
 
         @pl.when(step == middle - 1)
@@ -676,9 +684,19 @@
                 kv_in(k).wait_recv()
                 kv_share(k).start()
 
+        @pl.when(step == begin_old - 2)
+        def _():
+            q0_held[me] = sum_query(0)
+            gather_start(q0_held, tok_sems.at[2, 1], *tok)
+
+        @pl.when(step == begin_old - 1)
+        def _():
+            finish(q0_held, tok_sems.at[2, 1], *tok)
+
         return carry
 
     lax.fori_loop(0, n_head - 1, reduce_step, 0)
+    left = [(g, k) for g in range(n_head - 1 - begin_old, heads_here) for k in (0, 1)]
 
     last = n_head - 2
     for sub, way in lanes:
@@ -737,6 +755,10 @@
                 product2(chunk(step + 1, way))
         if step == middle - 1:
             product2(me_h)
+        if left:
+            old_half(*left.pop(0))
+    while left:
+        old_half(*left.pop(0))
     finish(squares, sq_sems, *head)
     mean = jnp.transpose(jnp.sum(squares[...], axis=0))[:, :1] / D
     factor = lax.rsqrt(mean + EPSILON)
@@ -803,13 +825,15 @@
         whole = held[...].astype(f32).reshape(-1, wide).astype(bf16)
         return both_of(whole, wo.at[:, :, pl.ds(low * DH, wide)], layer)
 
-    def project(layer, before):
+    def project(layer, before, beside=None):
         mix_group(layer, 0)
         mix_group(layer, 1)
         one, two = branch_of(layer, 0), branch_of(layer, 1)
         send, recv, held = b_send.at[layer], b_recv.at[layer], s_held.at[layer]
         pack(send, one[0] + two[0], one[1] + two[1])
         scatter_start(send, recv, head_sems.at[layer, 0], *head)
+        if beside is not None:
+            beside()
         recv[me_h] = send[me_h]
         finish(recv, head_sems.at[layer, 0], *head)
         total = jnp.sum(recv[...].astype(f32), axis=0)
@@ -824,23 +848,24 @@
             put_head(0, group, g, acc, top)
         send_group(0, group)
 
-    spread[pl.ds(0, tokens, stride=2), :] = fk[...].astype(f32)
-    spread[pl.ds(1, tokens, stride=2), :] = fv[...].astype(f32)
-    pages[0:own_pages] = spread[0 : 2 * tokens, :].reshape(own_pages, -1, DH).astype(bf16)
-    pages[own_pages:] = jnp.zeros((n_tok - own_pages, *pages.shape[1:]), bf16)
-    shift = lax.div(home_ref[0], pages_here)
-
-    def stage(peer, carry):
-        which = lax.rem(peer - shift - own_pages * me + 2 * n_tok * own_pages, n_tok)
-        outbox[peer] = pages[which]
-        return carry
-
-    lax.fori_loop(0, n_tok, stage, 0)
-    scatter_start(outbox, inbox, page_sems, *tok)
-    inbox[me] = outbox[me]
+    def send_pages():
+        spread[pl.ds(0, tokens, stride=2), :] = fk[...].astype(f32)
+        spread[pl.ds(1, tokens, stride=2), :] = fv[...].astype(f32)
+        pages[0:own_pages] = spread[0 : 2 * tokens, :].reshape(own_pages, -1, DH).astype(bf16)
+        pages[own_pages:] = jnp.zeros((n_tok - own_pages, *pages.shape[1:]), bf16)
+        shift = lax.div(home_ref[0], pages_here)
+
+        def stage(peer, carry):
+            which = lax.rem(peer - shift - own_pages * me + 2 * n_tok * own_pages, n_tok)
+            outbox[peer] = pages[which]
+            return carry
+
+        lax.fori_loop(0, n_tok, stage, 0)
+        scatter_start(outbox, inbox, page_sems, *tok)
+        inbox[me] = outbox[me]
 
     wo_in.wait()
-    project(0, state_ref)
+    project(0, state_ref, send_pages)
     send_query(1, unpack(s_held[0].astype(f32)))()
     ready = sum_query(1)
     cut = split_at * DH

time: 179 us -> 167 us (0.933)
  Pallas kernels: 176 us -> 164 us
    pallas_call x1, Pallas kernels: 172 us -> 160 us  [whole(): pl.pallas_call(functools.partial(whole_kernel, n_tok, n_head, side, subs,...]
where the time goes in v1:
time: 167 us
  Pallas kernels  164 us (98%)
    pallas_call x1, Pallas kernels, whole(): pl.pallas_call(functools.partial(whole_kernel, n_tok, n_head, side, subs,...  160 us
    pallas_call x1, Pallas kernels, place_pages(): pl.pallas_call(functools.partial(place_kernel, n_tok, own_pages), out_sha...  4.12 us

profile of v1, /device:TPU:1, one launch (start us, length us, event | category | flops | bytes accessed | tf_op | source)
XLA Modules:
  0.0 166.7 jit_solution(8234890176196763414)
XLA Ops:
  1.3 1.3 broadcast_in_dim.7.gain_hbm
  2.5 159.9 %whole.1 = (bf16[256,640]{1,0:T(8,128)(2,1)}, bf16[32,32,128]{2,1,0:T(8,128)(2,1)}, bf16[160,256]{1,0:T(8,128)(2,1)}) custom-call(s32[512]{0:T(512)} %home_ref.1, s32[1]{0:T(128)S(6)} %copy.17.len_hbm, s32[1,256]{1,0:T(1,128)} %bitcast.16, bf16[256,640]{1,0:T(8,128)(2,1)} %query_hbm.1, bf16[256,640]{1,0:T(8,128)(2,1)} %hid_hbm.1, ...), custom_call_target="tpu_custom_call" | custom-call | tf_op jit(solution)/shard_map/whole/pallas_call | solution.py:962
  162.5 4.1 %place_pages.1 = (bf16[8192,128]{1,0:T(8,128)(2,1)}, bf16[256,640]{1,0:T(8,128)(2,1)}, bf16[160,256]{1,0:T(8,128)(2,1)}) custom-call(s32[512]{0:T(512)} %home_ref.1, bf16[8192,128]{1,0:T(8,128)(2,1)} %bitcast.10, bf16[32,32,128]{2,1,0:T(8,128)(2,1)} %get-tuple-element.9.inbox_hbm, bf16[256,640]{1,0:T(8,128)(2,1)} %get-tuple-element.10.hid_hbm, ...), custom_call_target="tpu_custom_call" | custom-call | tf_op jit(solution)/shard_map/place_pages/pallas_call | solution.py:1136
